TPU v7x, 32 devices: a whole 2x2x4 slice. The times are simulated.
32 devices in a mesh: space: 8 (over z, core), spec: 4 (over y, x).
Axes of the slice: x: 2, y: 2, z: 4, core: 2. Of those that a mesh axis runs over, the one named last changes fastest.
Arguments:
- action: float32 [16, 24, 64, 512], P('spec', None, 'space'), may hold values from 0.1 to 1
- currents: float32 [2, 128, 1024], P(None, 'space', 'spec'), may hold values from -1.2 to 1.2
- wet: int32 [128, 1024], P('space', 'spec'), may hold values 0 or 1
- courant: float32 [16], replicated, may hold values from 0.1 to 0.35
- energy: float32 [16], replicated, may hold values from 0.3 to 3
- src: int32 [96, 512, 4], P('space'), may hold values from 4096 to 29695, as said below
- weights: float32 [96, 512, 4], P('space'), as said below
Outputs:
- new_action: float32 [16, 24, 64, 512], P('spec', None, 'space')
- new_currents: float32 [2, 128, 1024], P(None, 'space', 'spec')
Inputs may be any that keep to these rules, and one draw needn't show every extreme that they name: `src`: row e of block s refers to ocean rows 2 (e - 2) + 8 + j + a of the pair of ocean row blocks s and s + 1 (j 0 or 1 per wave cell, a the corner's row bit) and columns (2 x + i + b) mod 1024; the four corners of a cell are distinct; the two outer rows on each side of a block's lists refer to the same ocean cells, with the same weights, as the lists of the same wave rows in the neighbouring blocks. Positive; the 4 weights of a wave cell sum to one; rows that describe the same wave row are equal.
All inputs are finite; a program needn't handle non-finite values. No bound on the sum of `wet` on one device may be relied on, other than what follows from the above.
Results may differ from a plain program's by a relative error of at most 0.00009.
Values sent between devices are 32-bit elements; how exact they have to be, the bound alone decides.
No kernel may reach another device: no remote copies, remote signals or barrier semaphores. Data moves between devices by JAX's collectives and lax.ppermute only.
A program may use at most 128 MiB of HBM per device.

v0:
```python
import math
import jax
import jax.numpy as jnp
from jax import lax
from jax.sharding import PartitionSpec as P

drift_factor = 0.2
refract_factor = 1.5
damping = 0.95
force_gain = 0.5


def from_behind(block, axis, distance):
    devices = range(lax.axis_size(axis))
    route = [((i - distance) % len(devices), i) for i in devices]
    return lax.ppermute(block, axis, route)


def with_halo(cells, sides, width):
    for axis, dim in sides:
        count = lax.axis_size(axis)
        head = lax.slice_in_dim(cells, 0, width, axis=dim)
        tail = lax.slice_in_dim(cells, cells.shape[dim] - width, cells.shape[dim], axis=dim)
        cells = jnp.concatenate(
            [
                lax.ppermute(tail, axis, [(i, (i + 1) % count) for i in range(count)]),
                cells,
                lax.ppermute(head, axis, [((i + 1) % count, i) for i in range(count)]),
            ],
            axis=dim,
        )
    return cells


def advance(extended, speeds, flow, cosine, sine):
    east, north = (flow[0], flow[1])
    east_mid, north_mid = (east[1:-1], north[1:-1])
    grad_east_x = (jnp.roll(east_mid, -1, 1) - jnp.roll(east_mid, 1, 1)) * 0.5
    grad_north_x = (jnp.roll(north_mid, -1, 1) - jnp.roll(north_mid, 1, 1)) * 0.5
    grad_east_y = (east[2:] - east[:-2]) * 0.5
    grad_north_y = (north[2:] - north[:-2]) * 0.5
    cos3, sin3 = (cosine[:, None, None], sine[:, None, None])
    turn = refract_factor * (
        sin3 * cos3 * (grad_east_x - grad_north_y)[None]
        + sin3 * sin3 * grad_east_y[None]
        - cos3 * cos3 * grad_north_x[None]
    )
    speed_four = speeds[:, None, None, None]
    centre = extended[:, :, 1:-1]
    speed_x = speed_four * cos3[None] + drift_factor * east_mid[None, None]
    face_x = jnp.maximum(speed_x, 0.0) * centre + jnp.minimum(
        jnp.roll(speed_x, -1, 3), 0.0
    ) * jnp.roll(centre, -1, 3)
    speed_y = speed_four * sin3[None] + drift_factor * north[None, None]
    face_y = (
        jnp.maximum(speed_y[:, :, :-1], 0.0) * extended[:, :, :-1]
        + jnp.minimum(speed_y[:, :, 1:], 0.0) * extended[:, :, 1:]
    )
    face_turn = jnp.maximum(turn, 0.0)[None] * centre + jnp.minimum(jnp.roll(turn, -1, 0), 0.0)[
        None
    ] * jnp.roll(centre, -1, 1)
    return (
        centre
        - (face_x - jnp.roll(face_x, 1, 3))
        - (face_y[:, :, 1:] - face_y[:, :, :-1])
        - (face_turn - jnp.roll(face_turn, 1, 1))
    )


def stencil_tables(src, weights, ocean_cols, wave_rows):
    list_rows = src.shape[0]
    columns = src.shape[1]
    base_row = 2 * (jnp.arange(list_rows, dtype=jnp.int32) - 2) + wave_rows
    row_offset = src // ocean_cols - base_row[:, None, None]
    col_offset = (
        src % ocean_cols - 2 * jnp.arange(columns, dtype=jnp.int32)[None, :, None]
    ) % ocean_cols
    tables = []
    for step_row in range(3):
        for step_col in range(3):
            hit = jnp.logical_and(row_offset == step_row, col_offset == step_col)
            tables.append(jnp.sum(jnp.where(hit, weights, 0.0), axis=-1))
    return tables


def per_device(action, currents, wet, courant, energy, src, weights):
    wet_float = wet.astype(jnp.float32)
    masked = currents * wet_float[None]
    row_local = lax.all_gather(masked, "spec", axis=2, tiled=True)
    row_next = from_behind(row_local, "space", -1)
    ocean_rows = row_local.shape[1]
    ocean_cols = row_local.shape[2]
    wave_rows = action.shape[2]
    columns = src.shape[1]
    list_rows = src.shape[0]
    paired = jnp.concatenate([row_local, row_next], axis=1)
    tables = stencil_tables(src, weights, ocean_cols, wave_rows)
    first_row = wave_rows - 4
    window = paired[:, first_row : first_row + 2 * (list_rows + 1)].reshape(
        2, list_rows + 1, 2, columns, 2
    )
    drift = jnp.zeros((2, list_rows, columns), jnp.float32)
    for step_row in range(3):
        for step_col in range(3):
            lifted = window[
                :, step_row // 2 : step_row // 2 + list_rows, step_row % 2, :, step_col % 2
            ]
            if step_col == 2:
                lifted = jnp.roll(lifted, -1, 2)
            drift = drift + tables[3 * step_row + step_col][None] * lifted
    count_freq = action.shape[0]
    directions = action.shape[1]
    total_freq = count_freq * lax.axis_size("spec")
    start = lax.axis_index("spec") * count_freq
    freq_index = start + jnp.arange(count_freq, dtype=jnp.int32)
    speed_local = lax.dynamic_slice_in_dim(courant, start, count_freq)
    energy_local = lax.dynamic_slice_in_dim(energy, start, count_freq)
    angles = 2.0 * math.pi * (jnp.arange(directions, dtype=jnp.float32) + 0.5) / directions
    cosine, sine = (jnp.cos(angles), jnp.sin(angles))
    field = action
    for substep in range(2):
        extended = with_halo(field, (("space", 2),), 1)
        field = advance(extended, speed_local, drift[:, 1:-1], cosine, sine)
    ratio = 0.5 + 0.5 * freq_index.astype(jnp.float32) / (total_freq - 1)
    amplitude = energy_local / math.sqrt(directions * total_freq)
    coef = jnp.stack(
        [
            amplitude[:, None] * (ratio[:, None] * (cosine * cosine)[None] + ratio[:, None] - 0.5),
            amplitude[:, None] * (ratio[:, None] * (sine * sine)[None] + ratio[:, None] - 0.5),
            amplitude[:, None] * ratio[:, None] * (sine * cosine)[None],
        ]
    )
    stress = jnp.einsum("kfd,fdrx->krx", coef, field, precision=lax.Precision.HIGHEST)
    stress = lax.psum(stress, "spec")
    rimmed = with_halo(stress, (("space", 1),), 1)
    middle_stress = rimmed[:, 1:-1]
    grad_x = (jnp.roll(middle_stress, -1, 2) - jnp.roll(middle_stress, 1, 2)) * 0.5
    grad_y = (rimmed[:, 2:] - rimmed[:, :-2]) * 0.5
    force = jnp.stack([-(grad_x[0] + grad_y[2]), -(grad_x[2] + grad_y[1])])
    grid = jnp.zeros((2, wave_rows + 1, 2, columns, 2), jnp.float32)
    for step_row in range(3):
        for step_col in range(3):
            placed = tables[3 * step_row + step_col][2 : 2 + wave_rows][None] * force
            if step_col == 2:
                placed = jnp.roll(placed, 1, 2)
            grid = grid.at[
                :, step_row // 2 : step_row // 2 + wave_rows, step_row % 2, :, step_col % 2
            ].add(placed)
    flat_grid = grid.reshape(2, 2 * (wave_rows + 1), ocean_cols)
    below_pad = 2 * ocean_rows - wave_rows - 2 * (wave_rows + 1)
    pair_force = jnp.pad(flat_grid, ((0, 0), (wave_rows, below_pad), (0, 0)))
    width = currents.shape[2]
    share = lax.dynamic_slice_in_dim(pair_force, lax.axis_index("spec") * width, width, 2)
    lower = share[:, :ocean_rows]
    upper = share[:, ocean_rows:]
    below = from_behind(upper, "space", 1)
    pushed = lower + below
    updated = wet_float[None] * (damping * currents + force_gain * pushed)
    return (field, updated)


def solution(mesh):
    in_specs = (
        P("spec", None, "space", None),
        P(None, "space", "spec"),
        P("space", "spec"),
        P(),
        P(),
        P("space", None, None),
        P("space", None, None),
    )
    out_specs = (P("spec", None, "space", None), P(None, "space", "spec"))
    return jax.shard_map(
        per_device, mesh=mesh, in_specs=in_specs, out_specs=out_specs, check_vma=False
    )
```

profile of v0, /device:TPU:0, one launch (start us, length us, event | category | flops | bytes accessed | tf_op | source)
XLA Modules:
  0.0 138.4 jit_solution(14236402526247451844)
XLA Ops:
  0.6 0.7 convert_element_type.12
  1.4 0.8 copy_multiply_fusion
  2.1 9.9 %all_gather.3 = f32[2,16,1024]{2,0,1:T(2,128)S(1)} all-gather(f32[2,16,256]{2,0,1:T(2,128)S(1)} %copy_multiply_fusion), channel_id=1, replica_groups=mesh['space'=8,'spec'=4] {'spec'}, dimensions={2}, use_global_device_ids=true | all-gather | bytes 163840 | tf_op jit(solution)/shard_map/all_gather | solution.py:89
  12.1 1.1 collective-permute-start
  13.2 2.3 %copy.134 = f32[4,24,8,512]{3,1,2,0:T(8,128)S(1)} copy(f32[4,24,8,512]{3,2,1,0:T(8,128)} %param.25) | data formatting | bytes 3145728 | tf_op args[0]
  15.5 0.9 fusion.50
  16.4 3.5 %collective-permute-start.2 = (f32[4,24,1,512]{3,1,2,0:T(8,128)}, f32[4,24,1,512]{3,1,2,0:T(8,128)}, u32[]{:S(2)}, u32[]{:S(2)}) collective-permute-start(f32[4,24,1,512]{3,1,2,0:T(8,128)} %get-tuple-element.155), channel_id=1, source_target_pairs={{4,0},{8,4},{12,8},{16,12},{20,16},{24,20},{28,24},{0,28},{5,1},{9... | collective-permute-start | bytes 589832 | tf_op jit(solution)/shard_map/ppermute | solution.py:28
  20.3 0.3 broadcast_compare_fusion.6
  20.7 0.7 broadcast_multiply_fusion.5
  21.4 0.7 broadcast_multiply_fusion.7
  22.0 0.7 add_multiply_fusion.2
  22.7 0.7 select_reduce_fusion.8
  23.5 0.5 slice.776
  23.9 1.4 %slice.802 = f32[4,23,8,512]{3,1,2,0:T(8,128)} slice(f32[4,24,8,512]{3,1,2,0:T(8,128)S(1)} %copy.134), slice={[0:4], [1:24], [0:8], [0:512]} | slice | bytes 3014656 | tf_op jit(solution)/shard_map/jit(_roll_static)/slice | solution.py:61
  25.5 0.6 slice.830
  26.1 0.6 slice.838
  26.7 0.6 slice.846
  27.3 0.6 slice.817
  27.9 0.6 slice.828
  28.5 0.6 slice.834
  29.1 0.6 slice.836
  29.7 0.6 slice.842
  30.3 0.6 slice.844
  30.9 0.7 pad_maximum_fusion.6
  31.6 1.0 pad_maximum_fusion
  32.6 19.8 %reshape.996 = f32[2,13,2,512,2]{4,3,0,2,1:T(8,128)} reshape(f32[2,26,1024]{2,0,1:T(2,128)S(1)} %pad_maximum_fusion) | data formatting | bytes 425984 | tf_op jit(solution)/shard_map/reshape | solution.py:99
  52.4 21.7 %slice_reduce_fusion.4 = (f32[2,12,512]{2,0,1:T(2,128)S(1)}, f32[2,12,512]{2,0,1:T(2,128)S(1)}, f32[2,12,512]{2,0,1:T(2,128)S(1)}, f32[2,12,512]{2,0,1:T(2,128)S...) fusion(f32[2,13,2,512,2]{4,3,0,2,1:T(8,128)} %reshape.996), kind=kLoop, calls=%fused_computation.4 | loop fusion | bytes 589824 | tf_op jit(solution)/shard_map/slice | solution.py:105
  74.1 0.1 slice.763
  74.2 0.1 slice.767
  74.4 0.1 slice.771
  74.5 0.2 fusion.24
  75.1 0.1 fusion.37
  75.4 0.2 broadcast_maximum_fusion
  75.7 0.3 broadcast_add_fusion.1
  76.0 0.5 slice.774
  76.6 0.8 copy-done.2
  77.4 0.5 copy-done.3
  77.9 0.2 slice-done
  78.0 1.9 %fusion.8 = (f32[4,24,8,512]{3,1,2,0:T(8,128)S(1)}, f32[4,24,8,512]{3,1,2,0:T(8,128)S(1)}) fusion(f32[4,1,8,512]{3,1,2,0:T(1,128)S(1)} %copy.144, f32[4,23,8,512]{3,1,2,0:T(8,128)S(1)} %copy-done.3, f32[24,8,512]{2,0,1:T(8,128)S(1)} %maximum_minimum_fusion.1, f32[24,8,512]{2,0,1:T(8,128)S(1)} %get-tuple-element.171, f32[4,24,8,512]{3,2,1,0:T(8,128)S(1)} %copy-done.2, ...), kind=kLoop, calls=%fused_computation.26 | loop fusion | flops 4718592 | bytes 10240384 | tf_op jit(solution)/shard_map/add | solution.py:59
  79.9 0.2 slice.778
  80.2 0.3 broadcast_add_fusion
  80.6 0.8 copy-done.1
  81.3 1.5 %fusion = f32[4,24,9,512]{3,1,2,0:T(8,128)S(1)} fusion(f32[4,24,8,512]{3,1,2,0:T(8,128)S(1)} %copy-done.1, f32[4,24,1,512]{3,1,2,0:T(8,128)} %collective-permute-done.1, f32[4,24,1,512]{3,1,2,0:T(8,128)} %collective-permute-done.2, f32[4,24,10,512]{3,1,2,0:T(8,128)S(1)} %broadcast_add_fusion), kind=kLoop, calls=%fused_computation.9 | loop fusion | flops 3096576 | bytes 7274496 | tf_op jit(solution)/shard_map/add | solution.py:56
  82.9 2.4 %fusion.5 = f32[4,24,8,512]{3,1,2,0:T(8,128)S(1)} fusion(f32[4,24,9,512]{3,1,2,0:T(8,128)S(1)} %fusion, f32[4,24,8,512]{3,1,2,0:T(8,128)S(1)} %get-tuple-element.154, f32[4,24,8,511]{3,1,2,0:T(8,128)S(1)} %bitcast.61, f32[4,24,8,1]{3,1,2,0:T(8,128)S(1)} %slice.778, f32[4,24,8,512]{3,1,2,0:T(8,128)S(1)} %get-tuple-element.153, ...), kind=kLoop, calls=%fused_computation.19 | loop fusion | flops 3145728 | bytes 12582912 | tf_op jit(solution)/shard_map/sub | solution.py:63
  85.3 0.5 slice.805
  85.8 0.3 slice.813
  86.2 3.5 %collective-permute-start.4 = (f32[4,24,1,512]{3,1,2,0:T(8,128)S(1)}, f32[4,24,1,512]{3,1,2,0:T(8,128)S(1)}, u32[]{:S(2)}, u32[]{:S(2)}) collective-permute-start(f32[4,24,1,512]{3,1,2,0:T(8,128)S(1)} %get-tuple-element.151), channel_id=1, source_target_pairs={{4,0},{8,4},{12,8},{16,12},{20,16},{24,20},{28,24},{0,28},{5,1},{9... | collective-permute-start | bytes 589832 | tf_op jit(solution)/shard_map/ppermute | solution.py:28
  89.8 1.1 fusion.11
  90.8 0.2 slice.807
  91.1 3.4 %collective-permute-done.3 = f32[4,24,1,512]{3,1,2,0:T(8,128)S(1)} collective-permute-done((f32[4,24,1,512]{3,1,2,0:T(8,128)S(1)}, f32[4,24,1,512]{3,1,2,0:T(8,128)S(1)}, u32[]{:S(2)}, u32[]{:S(2)}) %collective-permute-start.3) | collective-permute-done | bytes 196640 | tf_op jit(solution)/shard_map/ppermute | solution.py:26
  94.6 0.5 fusion.1
  95.0 1.4 %fusion.3 = f32[4,24,8,512]{3,1,2,0:T(8,128)S(1)} fusion(f32[4,24,9,512]{3,1,2,0:T(8,128)S(1)} %fusion.1, f32[4,24,8,512]{3,1,2,0:T(8,128)S(1)} %fusion.5, f32[4,24,8,512]{3,1,2,0:T(8,128)S(1)} %get-tuple-element.150, f32[4,24,8,511]{3,1,2,0:T(8,128)S(1)} %bitcast.60, f32[4,24,8,1]{3,1,2,0:T(8,128)S(1)} %slice.807, ...), kind=kLoop, calls=%fused_computation.16 | loop fusion | flops 3145728 | bytes 12582912 | tf_op jit(solution)/shard_map/sub | solution.py:63
  96.5 0.9 convolution_bitcast_fusion
  97.4 16.0 %psum.7 = f32[3,8,512]{2,0,1:T(4,128)S(1)} all-reduce(f32[3,8,512]{2,0,1:T(4,128)S(1)} %convolution_bitcast_fusion), channel_id=1, replica_groups=mesh['space'=8,'spec'=4] {'spec'}, use_global_device_ids=true, to_apply=%region_9.10 | all-reduce | flops 12288 | bytes 98304 | tf_op jit(solution)/shard_map/psum | solution.py:134
  113.7 0.5 collective-permute-start.6
  114.2 0.1 fusion.18
  114.3 0.7 collective-permute-done.5
  115.1 3.6 %collective-permute-done.6 = f32[3,1,512]{2,0,1:T(4,128)S(1)} collective-permute-done((f32[3,1,512]{2,0,1:T(4,128)S(1)}, f32[3,1,512]{2,0,1:T(4,128)S(1)}, u32[]{:S(2)}, u32[]{:S(2)}) %collective-permute-start.6) | collective-permute-done | bytes 6176 | tf_op jit(solution)/shard_map/ppermute | solution.py:26
  119.2 0.1 fusion.32
  119.8 5.0 %copy.148 = f32[2,9,2,512,2]{4,3,0,2,1:T(8,128)} copy(f32[2,9,2,512,2]{3,0,1,4,2:T(2,128)S(1)} %fusion.26) | data formatting | bytes 294912 | tf_op jit(solution)/shard_map/scatter-add | solution.py:148
  124.8 7.7 %reshape.1000 = f32[2,18,1024]{2,0,1:T(2,128)S(1)} reshape(f32[2,9,2,512,2]{4,3,0,2,1:T(8,128)} %copy.148) | data formatting | bytes 294912 | tf_op jit(solution)/shard_map/reshape | solution.py:149
  132.6 2.1 %copy.149 = f32[4,24,8,512]{3,2,1,0:T(8,128)} copy(f32[4,24,8,512]{3,1,2,0:T(8,128)S(1)} %fusion.3) | data formatting | bytes 3145728
  134.7 3.1 %collective-permute-done.7 = f32[2,16,256]{2,0,1:T(2,128)S(1)} collective-permute-done((f32[2,16,256]{2,0,1:T(2,128)S(1)}, f32[2,16,256]{2,0,1:T(2,128)S(1)}, u32[]{:S(2)}, u32[]{:S(2)}) %collective-permute-start.7) | collective-permute-done | bytes 32800 | tf_op jit(solution)/shard_map/ppermute | solution.py:16
  137.8 0.6 copy.150
  (128 shorter events, 2.9 us)
Async XLA Ops:
  12.1 8.0 %copy-start.31 = (f32[16]{0:T(128)S(1)}, f32[16]{0:T(128)}, u32[]{:S(2)}) copy-start(f32[16]{0:T(128)} %param.28) | copy-start | bytes 196
  12.1 8.1 %copy-start.30 = (f32[16]{0:T(128)S(1)}, f32[16]{0:T(128)}, u32[]{:S(2)}) copy-start(f32[16]{0:T(128)} %param.29) | copy-start | bytes 196
  12.1 8.2 %copy-start.11 = (s32[12,512,4]{1,2,0:T(4,128)S(1)}, s32[12,512,4]{1,2,0:T(4,128)}, u32[]{:S(2)}) copy-start(s32[12,512,4]{1,2,0:T(4,128)} %param.30) | copy-start | bytes 294916
  12.1 10.6 %copy-start.12 = (f32[12,512,4]{1,2,0:T(4,128)S(1)}, f32[12,512,4]{1,2,0:T(4,128)}, u32[]{:S(2)}) copy-start(f32[12,512,4]{1,2,0:T(4,128)} %param.31) | copy-start | bytes 294916
  12.1 19.5 %collective-permute-start = (f32[2,16,1024]{2,0,1:T(2,128)S(1)}, f32[2,16,1024]{2,0,1:T(2,128)}, u32[]{:S(2)}, u32[]{:S(2)}) collective-permute-start(f32[2,16,1024]{2,0,1:T(2,128)S(1)} %all_gather.3), channel_id=1, source_target_pairs={{4,0},{8,4},{12,8},{16,12},{20,16},{24,20},{28,24},{0,28},{5,1},{9... | collective-permute-start | bytes 393224 | tf_op jit(solution)/shard_map/ppermute | solution.py:16
  15.5 9.9 %copy-start = (f32[4,24,8,512]{3,1,2,0:T(8,128)}, f32[4,24,8,512]{3,1,2,0:T(8,128)S(1)}, u32[]{:S(2)}) copy-start(f32[4,24,8,512]{3,1,2,0:T(8,128)S(1)} %copy.134) | copy-start | bytes 4718596
  16.4 64.2 %collective-permute-start.1 = (f32[4,24,1,512]{3,1,2,0:T(8,128)}, f32[4,24,1,512]{3,1,2,0:T(8,128)}, u32[]{:S(2)}, u32[]{:S(2)}) collective-permute-start(f32[4,24,1,512]{3,1,2,0:T(8,128)} %get-tuple-element.156), channel_id=1, source_target_pairs={{0,4},{4,8},{8,12},{12,16},{16,20},{20,24},{24,28},{28,0},{1,5},{5... | collective-permute-start | bytes 589832 | tf_op jit(solution)/shard_map/ppermute | solution.py:26
  16.4 64.2 %collective-permute-start.2 = (f32[4,24,1,512]{3,1,2,0:T(8,128)}, f32[4,24,1,512]{3,1,2,0:T(8,128)}, u32[]{:S(2)}, u32[]{:S(2)}) collective-permute-start(f32[4,24,1,512]{3,1,2,0:T(8,128)} %get-tuple-element.155), channel_id=1, source_target_pairs={{4,0},{8,4},{12,8},{16,12},{20,16},{24,20},{28,24},{0,28},{5,1},{9... | collective-permute-start | bytes 589832 | tf_op jit(solution)/shard_map/ppermute | solution.py:28
  20.0 2.7 %copy-start.24 = (f32[24]{0:T(128)}, f32[24]{0:T(128)S(1)}, u32[]{:S(2)}) copy-start(f32[24]{0:T(128)S(1)} %get-tuple-element.196) | copy-start | bytes 292
  20.0 2.7 %copy-start.28 = (f32[24]{0:T(128)}, f32[24]{0:T(128)S(1)}, u32[]{:S(2)}) copy-start(f32[24]{0:T(128)S(1)} %get-tuple-element.197) | copy-start | bytes 292
  20.1 2.6 %copy-start.26 = (f32[24]{0:T(128)}, f32[24]{0:T(128)S(1)}, u32[]{:S(2)}) copy-start(f32[24]{0:T(128)S(1)} %fusion.46) | copy-start | bytes 292
  23.4 4.4 %copy-start.6 = (f32[12,512]{1,0:T(8,128)}, f32[12,512]{1,0:T(8,128)S(1)}, u32[]{:S(2)}) copy-start(f32[12,512]{1,0:T(8,128)S(1)} %get-tuple-element.141) | copy-start | bytes 73732
  23.4 5.6 %copy-start.4 = (f32[12,512]{1,0:T(8,128)}, f32[12,512]{1,0:T(8,128)S(1)}, u32[]{:S(2)}) copy-start(f32[12,512]{1,0:T(8,128)S(1)} %get-tuple-element.140) | copy-start | bytes 73732
  23.4 6.8 %copy-start.8 = (f32[12,512]{1,0:T(8,128)}, f32[12,512]{1,0:T(8,128)S(1)}, u32[]{:S(2)}) copy-start(f32[12,512]{1,0:T(8,128)S(1)} %get-tuple-element.142) | copy-start | bytes 73732
  23.9 1.5 %slice-start.1 = ((f32[4,24,8,512]{3,2,1,0:T(8,128)}), f32[4,1,8,512]{3,2,1,0:T(8,128)S(1)}, s32[]{:S(2)}) async-start(f32[4,24,8,512]{3,2,1,0:T(8,128)} %param.25), calls=%async_computation.1 | async-start | bytes 131072 | tf_op jit(solution)/shard_map/jit(_roll_static)/slice | solution.py:61
  52.4 22.1 %copy-start.5 = (f32[12,512]{1,0:T(8,128)S(1)}, f32[12,512]{1,0:T(8,128)}, u32[]{:S(2)}) copy-start(f32[12,512]{1,0:T(8,128)} %copy-done.4) | copy-start | bytes 73732
  52.4 22.1 %copy-start.7 = (f32[12,512]{1,0:T(8,128)S(1)}, f32[12,512]{1,0:T(8,128)}, u32[]{:S(2)}) copy-start(f32[12,512]{1,0:T(8,128)} %copy-done.6) | copy-start | bytes 73732
  52.4 22.1 %copy-start.9 = (f32[12,512]{1,0:T(8,128)S(1)}, f32[12,512]{1,0:T(8,128)}, u32[]{:S(2)}) copy-start(f32[12,512]{1,0:T(8,128)} %copy-done.8) | copy-start | bytes 73732
  74.1 1.3 copy-start.25
  74.1 1.3 copy-start.27
  74.1 1.3 copy-start.29
  74.5 1.2 copy-start.22
  76.0 1.4 %copy-start.2 = (f32[4,24,8,512]{3,2,1,0:T(8,128)S(1)}, f32[4,24,8,512]{3,2,1,0:T(8,128)}, u32[]{:S(2)}) copy-start(f32[4,24,8,512]{3,2,1,0:T(8,128)} %param.25) | copy-start | bytes 4718596
  76.0 1.9 %copy-start.3 = (f32[4,23,8,512]{3,1,2,0:T(8,128)S(1)}, f32[4,23,8,512]{3,1,2,0:T(8,128)}, u32[]{:S(2)}) copy-start(f32[4,23,8,512]{3,1,2,0:T(8,128)} %slice.802) | copy-start | bytes 4521988
  76.5 1.6 %slice-start = ((f32[4,24,8,512]{3,1,2,0:T(8,128)}), f32[4,24,8,1]{3,1,2,0:T(8,128)S(1)}, s32[]{:S(2)}) async-start(f32[4,24,8,512]{3,1,2,0:T(8,128)} %copy-done), calls=%async_computation | async-start | bytes 786432 | tf_op jit(solution)/shard_map/jit(_roll_static)/slice | solution.py:53
  78.0 2.2 %copy-start.23 = (f32[4,24]{1,0:T(4,128)S(1)}, f32[4,24]{1,0:T(4,128)}, u32[]{:S(2)}) copy-start(f32[4,24]{1,0:T(4,128)} %get-tuple-element.190) | copy-start | bytes 1156
  79.9 1.4 %copy-start.1 = (f32[4,24,8,512]{3,1,2,0:T(8,128)S(1)}, f32[4,24,8,512]{3,1,2,0:T(8,128)}, u32[]{:S(2)}) copy-start(f32[4,24,8,512]{3,1,2,0:T(8,128)} %copy-done) | copy-start | bytes 4718596
  86.2 8.4 %collective-permute-start.3 = (f32[4,24,1,512]{3,1,2,0:T(8,128)S(1)}, f32[4,24,1,512]{3,1,2,0:T(8,128)S(1)}, u32[]{:S(2)}, u32[]{:S(2)}) collective-permute-start(f32[4,24,1,512]{3,1,2,0:T(8,128)S(1)} %get-tuple-element.152), channel_id=1, source_target_pairs={{0,4},{4,8},{8,12},{12,16},{16,20},{20,24},{24,28},{28,0},{1,5},{5... | collective-permute-start | bytes 589832 | tf_op jit(solution)/shard_map/ppermute | solution.py:26
  86.2 8.3 %collective-permute-start.4 = (f32[4,24,1,512]{3,1,2,0:T(8,128)S(1)}, f32[4,24,1,512]{3,1,2,0:T(8,128)S(1)}, u32[]{:S(2)}, u32[]{:S(2)}) collective-permute-start(f32[4,24,1,512]{3,1,2,0:T(8,128)S(1)} %get-tuple-element.151), channel_id=1, source_target_pairs={{4,0},{8,4},{12,8},{16,12},{20,16},{24,20},{28,24},{0,28},{5,1},{9... | collective-permute-start | bytes 589832 | tf_op jit(solution)/shard_map/ppermute | solution.py:28
  96.5 22.3 %copy-start.19 = (f32[8,512]{1,0:T(8,128)S(1)}, f32[8,512]{1,0:T(8,128)}, u32[]{:S(2)}) copy-start(f32[8,512]{1,0:T(8,128)} %slice.830) | copy-start | bytes 49156
  96.5 22.3 %copy-start.20 = (f32[8,512]{1,0:T(8,128)S(1)}, f32[8,512]{1,0:T(8,128)}, u32[]{:S(2)}) copy-start(f32[8,512]{1,0:T(8,128)} %slice.838) | copy-start | bytes 49156
  96.5 22.3 %copy-start.21 = (f32[8,512]{1,0:T(8,128)S(1)}, f32[8,512]{1,0:T(8,128)}, u32[]{:S(2)}) copy-start(f32[8,512]{1,0:T(8,128)} %slice.846) | copy-start | bytes 49156
  96.5 22.6 %copy-start.18 = (f32[8,512]{1,0:T(8,128)S(1)}, f32[8,512]{1,0:T(8,128)}, u32[]{:S(2)}) copy-start(f32[8,512]{1,0:T(8,128)} %slice.817) | copy-start | bytes 49156
  96.5 22.7 %copy-start.17 = (f32[8,512]{1,0:T(8,128)S(1)}, f32[8,512]{1,0:T(8,128)}, u32[]{:S(2)}) copy-start(f32[8,512]{1,0:T(8,128)} %slice.828) | copy-start | bytes 49156
  96.5 22.8 %copy-start.16 = (f32[8,512]{1,0:T(8,128)S(1)}, f32[8,512]{1,0:T(8,128)}, u32[]{:S(2)}) copy-start(f32[8,512]{1,0:T(8,128)} %slice.834) | copy-start | bytes 49156
  96.5 22.9 %copy-start.15 = (f32[8,512]{1,0:T(8,128)S(1)}, f32[8,512]{1,0:T(8,128)}, u32[]{:S(2)}) copy-start(f32[8,512]{1,0:T(8,128)} %slice.836) | copy-start | bytes 49156
  96.5 23.0 %copy-start.14 = (f32[8,512]{1,0:T(8,128)S(1)}, f32[8,512]{1,0:T(8,128)}, u32[]{:S(2)}) copy-start(f32[8,512]{1,0:T(8,128)} %slice.842) | copy-start | bytes 49156
  96.5 23.1 %copy-start.13 = (f32[8,512]{1,0:T(8,128)S(1)}, f32[8,512]{1,0:T(8,128)}, u32[]{:S(2)}) copy-start(f32[8,512]{1,0:T(8,128)} %slice.844) | copy-start | bytes 49156
  113.7 1.4 %collective-permute-start.5 = (f32[3,1,512]{2,0,1:T(4,128)S(1)}, f32[3,1,512]{2,0,1:T(4,128)S(1)}, u32[]{:S(2)}, u32[]{:S(2)}) collective-permute-start(f32[3,1,512]{2,0,1:T(4,128)S(1)} %get-tuple-element.169), channel_id=1, source_target_pairs={{4,0},{8,4},{12,8},{16,12},{20,16},{24,20},{28,24},{0,28},{5,1},{9... | collective-permute-start | bytes 18440 | tf_op jit(solution)/shard_map/ppermute | solution.py:28
  113.7 4.9 %collective-permute-start.6 = (f32[3,1,512]{2,0,1:T(4,128)S(1)}, f32[3,1,512]{2,0,1:T(4,128)S(1)}, u32[]{:S(2)}, u32[]{:S(2)}) collective-permute-start(f32[3,1,512]{2,0,1:T(4,128)S(1)} %get-tuple-element.170), channel_id=1, source_target_pairs={{0,4},{4,8},{8,12},{12,16},{16,20},{20,24},{24,28},{28,0},{1,5},{5... | collective-permute-start | bytes 18440 | tf_op jit(solution)/shard_map/ppermute | solution.py:26
  132.5 5.2 %copy-start.10 = (f32[2,16,256]{2,1,0:T(8,128)S(1)}, f32[2,16,256]{2,1,0:T(8,128)}, u32[]{:S(2)}) copy-start(f32[2,16,256]{2,1,0:T(8,128)} %param.26) | copy-start | bytes 98308
  132.6 5.2 %collective-permute-start.7 = (f32[2,16,256]{2,0,1:T(2,128)S(1)}, f32[2,16,256]{2,0,1:T(2,128)S(1)}, u32[]{:S(2)}, u32[]{:S(2)}) collective-permute-start(f32[2,16,256]{2,0,1:T(2,128)S(1)} %pad_dynamic-slice_fusion.1), channel_id=1, source_target_pairs={{28,0},{0,4},{4,8},{8,12},{12,16},{16,20},{20,24},{24,28},{29,1},{... | collective-permute-start | bytes 98312 | tf_op jit(solution)/shard_map/ppermute | solution.py:16
where the time goes:
time: 139 us; the launch traced here: 138 us
  local copies, waits for them, and re-layouts  72.9 us (52%)
  blocking collectives  26 us (19%)
  other arithmetic  17.6 us (13%)
  waiting for transfers between devices  10.8 us (8%)
  starting transfers between devices  8.79 us (6%)
  between operations  1.45 us (1%)
    slice x1, local copies, waits for them, and re-layouts, per_device(): window[:, step_row // 2:step_row // 2 + list_rows, step_row % 2, :, step_...  21.7 us
    reshape x1, local copies, waits for them, and re-layouts, per_device(): paired[:, first_row:first_row + 2 * (list_rows + 1)]  19.8 us
    psum x1, blocking collectives, per_device(): stress = lax.psum(stress, 'spec')  16 us
    all_gather x1, blocking collectives, per_device(): row_local = lax.all_gather(masked, 'spec', axis=2, tiled=True)  9.94 us
    reshape x1, local copies, waits for them, and re-layouts, per_device(): flat_grid = grid.reshape(2, 2 * (wave_rows + 1), ocean_cols)  7.66 us
    unnamed x72, local copies, waits for them, and re-layouts  7.16 us
    ppermute x3, starting transfers between devices, with_halo(): lax.ppermute(head, axis, [((i + 1) % count, i) for i in range(count)])  7.11 us
    ppermute x3, waiting for transfers between devices, with_halo(): lax.ppermute(tail, axis, [(i, (i + 1) % count) for i in range(count)])  7.02 us
  transfers between devices with their start and end apart: 8, of which 4 were waited for; matrix products, arithmetic and copies ran while one was open for 47% of the time, Pallas kernels for 0%

commit v1 on v0

--- a/solution.py
+++ b/solution.py
@@ -8,6 +8,17 @@
 refract_factor = 1.5
 damping = 0.95
 force_gain = 0.5
+
+
+def gather_by_hops(shard, axis, dim):
+    size = lax.axis_size(axis)
+    right = [(i, (i + 1) % size) for i in range(size)]
+    parts = [shard]
+    for far in range(1, size):
+        parts = [lax.ppermute(parts[0], axis, right), *parts]
+    whole = jnp.concatenate(parts, axis=dim)
+    offset = (lax.axis_index(axis) + 1) * parts[-1].shape[dim]
+    return jnp.roll(whole, offset, axis=dim)
 
 
 def from_behind(block, axis, distance):
@@ -86,7 +97,7 @@
 def per_device(action, currents, wet, courant, energy, src, weights):
     wet_float = wet.astype(jnp.float32)
     masked = currents * wet_float[None]
-    row_local = lax.all_gather(masked, "spec", axis=2, tiled=True)
+    row_local = gather_by_hops(masked, "spec", 2)
     row_next = from_behind(row_local, "space", -1)
     ocean_rows = row_local.shape[1]
     ocean_cols = row_local.shape[2]

time: 139 us -> 143 us (1.029)
  blocking collectives: 26 us -> 14.8 us
  waiting for transfers between devices: 10.8 us -> 17.4 us
  starting transfers between devices: 8.79 us -> 12.9 us
  local copies, waits for them, and re-layouts: 72.9 us -> 75.9 us
    all_gather x1 -> x0, blocking collectives: 9.94 us -> none  [per_device(): row_local = lax.all_gather(masked, 'spec', axis=2, tiled=True)]
    ppermute x0 -> x3, waiting for transfers between devices: none -> 6.22 us  [gather_by_hops(): parts = [lax.ppermute(parts[0], axis, right), *parts]]
    ppermute x0 -> x3, starting transfers between devices: none -> 5.1 us  [gather_by_hops(): parts = [lax.ppermute(parts[0], axis, right), *parts]]
    slice x9, local copies, waits for them, and re-layouts: 5.42 us -> 8.45 us  [per_device(): placed = tables[3 * step_row + step_col][2:2 + wave_rows][None] * force]
    unnamed x72 -> x76, local copies, waits for them, and re-layouts: 7.16 us -> 7.23 us
  transfers between devices with their start and end apart: 8 -> 11, of which waited for: 4 -> 6; matrix products, arithmetic and copies ran while one was open for 47% -> 49% of each run, Pallas kernels for 0% -> 0%
where the time goes in v1:
time: 143 us; the launch traced here: 142 us
  local copies, waits for them, and re-layouts  75.9 us (53%)
  other arithmetic  19 us (13%)
  waiting for transfers between devices  17.4 us (12%)
  blocking collectives  14.8 us (10%)
  starting transfers between devices  12.9 us (9%)
  between operations  1.52 us (1%)
    slice x1, local copies, waits for them, and re-layouts, per_device(): window[:, step_row // 2:step_row // 2 + list_rows, step_row % 2, :, step_...  21.6 us
    reshape x1, local copies, waits for them, and re-layouts, per_device(): paired[:, first_row:first_row + 2 * (list_rows + 1)]  19.9 us
    psum x1, blocking collectives, per_device(): stress = lax.psum(stress, 'spec')  14.8 us
    slice x9, local copies, waits for them, and re-layouts, per_device(): placed = tables[3 * step_row + step_col][2:2 + wave_rows][None] * force  8.45 us
    reshape x1, local copies, waits for them, and re-layouts, per_device(): flat_grid = grid.reshape(2, 2 * (wave_rows + 1), ocean_cols)  7.66 us
    ppermute x3, waiting for transfers between devices, with_halo(): lax.ppermute(tail, axis, [(i, (i + 1) % count) for i in range(count)])  7.37 us
    unnamed x76, local copies, waits for them, and re-layouts  7.23 us
    ppermute x3, starting transfers between devices, with_halo(): lax.ppermute(head, axis, [((i + 1) % count, i) for i in range(count)])  6.64 us
  transfers between devices with their start and end apart: 11, of which 6 were waited for; matrix products, arithmetic and copies ran while one was open for 49% of the time, Pallas kernels for 0%

profile of v1, /device:TPU:0, one launch (start us, length us, event | category | flops | bytes accessed | tf_op | source)
XLA Modules:
  0.0 142.3 jit_solution(10562811540553478179)
XLA Ops:
  0.6 0.7 convert_element_type.12
  1.4 0.8 copy_multiply_fusion
  2.2 3.0 %collective-permute-start = (f32[2,16,256]{2,0,1:T(2,128)S(1)}, f32[2,16,256]{2,0,1:T(2,128)S(1)}, u32[]{:S(2)}, u32[]{:S(2)}) collective-permute-start(f32[2,16,256]{2,0,1:T(2,128)S(1)} %copy_multiply_fusion), channel_id=1, source_target_pairs={{0,1},{1,2},{2,3},{3,0},{4,5},{5,6},{6,7},{7,4},{8,9},{9,10},{10,1... | collective-permute-start | bytes 98312 | tf_op jit(solution)/shard_map/ppermute | solution.py:18
  5.2 2.3 %copy.134 = f32[4,24,8,512]{3,1,2,0:T(8,128)S(1)} copy(f32[4,24,8,512]{3,2,1,0:T(8,128)} %param.25) | data formatting | bytes 3145728 | tf_op args[0]
  7.6 0.8 fusion.50
  8.3 3.5 %collective-permute-start.5 = (f32[4,24,1,512]{3,1,2,0:T(8,128)}, f32[4,24,1,512]{3,1,2,0:T(8,128)}, u32[]{:S(2)}, u32[]{:S(2)}) collective-permute-start(f32[4,24,1,512]{3,1,2,0:T(8,128)} %get-tuple-element.155), channel_id=1, source_target_pairs={{4,0},{8,4},{12,8},{16,12},{20,16},{24,20},{28,24},{0,28},{5,1},{9... | collective-permute-start | bytes 589832 | tf_op jit(solution)/shard_map/ppermute | solution.py:39
  12.0 0.3 broadcast_compare_fusion.6
  12.6 0.7 add_multiply_fusion.2
  13.4 1.5 %collective-permute-start.1 = (f32[2,16,256]{2,0,1:T(2,128)S(1)}, f32[2,16,256]{2,0,1:T(2,128)S(1)}, u32[]{:S(2)}, u32[]{:S(2)}) collective-permute-start(f32[2,16,256]{2,0,1:T(2,128)S(1)} %collective-permute-done), channel_id=1, source_target_pairs={{0,1},{1,2},{2,3},{3,0},{4,5},{5,6},{6,7},{7,4},{8,9},{9,10},{10,1... | collective-permute-start | bytes 98312 | tf_op jit(solution)/shard_map/ppermute | solution.py:18
  14.9 0.7 broadcast_multiply_fusion.7
  15.5 2.7 %collective-permute-done.1 = f32[2,16,256]{2,0,1:T(2,128)S(1)} collective-permute-done((f32[2,16,256]{2,0,1:T(2,128)S(1)}, f32[2,16,256]{2,0,1:T(2,128)S(1)}, u32[]{:S(2)}, u32[]{:S(2)}) %collective-permute-start.1) | collective-permute-done | bytes 32800 | tf_op jit(solution)/shard_map/ppermute | solution.py:18
  18.2 0.6 collective-permute-start.2
  18.8 0.7 broadcast_multiply_fusion.5
  19.4 3.6 %collective-permute-done.2 = f32[2,16,256]{2,0,1:T(2,128)S(1)} collective-permute-done((f32[2,16,256]{2,0,1:T(2,128)S(1)}, f32[2,16,256]{2,0,1:T(2,128)S(1)}, u32[]{:S(2)}, u32[]{:S(2)}) %collective-permute-start.2) | collective-permute-done | bytes 32800 | tf_op jit(solution)/shard_map/ppermute | solution.py:18
  23.3 1.3 select_reduce_fusion.8
  24.6 0.5 slice.776
  25.1 1.4 %slice.802 = f32[4,23,8,512]{3,1,2,0:T(8,128)} slice(f32[4,24,8,512]{3,1,2,0:T(8,128)S(1)} %copy.134), slice={[0:4], [1:24], [0:8], [0:512]} | slice | bytes 3014656 | tf_op jit(solution)/shard_map/jit(_roll_static)/slice | solution.py:72
  26.6 0.6 slice.830
  27.2 0.6 slice.838
  27.8 0.6 slice.846
  28.4 0.6 slice.817
  29.0 1.4 slice.828
  30.4 1.4 slice.834
  31.7 1.4 slice.836
  33.1 0.6 slice.842
  33.7 1.4 slice.844
  35.1 1.3 pad_maximum_fusion.6
  36.3 1.0 pad_maximum_fusion
  37.3 19.9 %reshape.996 = f32[2,13,2,512,2]{4,3,0,2,1:T(8,128)} reshape(f32[2,26,1024]{2,0,1:T(2,128)S(1)} %pad_maximum_fusion) | data formatting | bytes 425984 | tf_op jit(solution)/shard_map/reshape | solution.py:110
  57.2 21.6 %slice_reduce_fusion.4 = (f32[2,12,512]{2,0,1:T(2,128)S(1)}, f32[2,12,512]{2,0,1:T(2,128)S(1)}, f32[2,12,512]{2,0,1:T(2,128)S(1)}, f32[2,12,512]{2,0,1:T(2,128)S...) fusion(f32[2,13,2,512,2]{4,3,0,2,1:T(8,128)} %reshape.996), kind=kLoop, calls=%fused_computation.4 | loop fusion | bytes 589824 | tf_op jit(solution)/shard_map/slice | solution.py:116
  78.9 0.1 slice.763
  79.3 0.2 fusion.24
  79.8 0.1 fusion.37
  80.2 0.2 broadcast_maximum_fusion
  80.5 0.3 broadcast_add_fusion.1
  80.8 0.5 slice.774
  81.4 0.8 copy-done.2
  82.2 0.5 copy-done.3
  82.6 0.2 slice-done
  82.8 1.9 %fusion.8 = (f32[4,24,8,512]{3,1,2,0:T(8,128)S(1)}, f32[4,24,8,512]{3,1,2,0:T(8,128)S(1)}) fusion(f32[4,1,8,512]{3,1,2,0:T(1,128)S(1)} %copy.144, f32[4,23,8,512]{3,1,2,0:T(8,128)S(1)} %copy-done.3, f32[24,8,512]{2,0,1:T(8,128)S(1)} %maximum_minimum_fusion.1, f32[24,8,512]{2,0,1:T(8,128)S(1)} %get-tuple-element.171, f32[4,24,8,512]{3,2,1,0:T(8,128)S(1)} %copy-done.2, ...), kind=kLoop, calls=%fused_computation.26 | loop fusion | flops 4718592 | bytes 10240384 | tf_op jit(solution)/shard_map/add | solution.py:70
  84.7 0.2 slice.778
  85.0 0.3 broadcast_add_fusion
  85.3 0.8 copy-done.1
  86.1 1.5 %fusion = f32[4,24,9,512]{3,1,2,0:T(8,128)S(1)} fusion(f32[4,24,8,512]{3,1,2,0:T(8,128)S(1)} %copy-done.1, f32[4,24,1,512]{3,1,2,0:T(8,128)} %collective-permute-done.4, f32[4,24,1,512]{3,1,2,0:T(8,128)} %collective-permute-done.5, f32[4,24,10,512]{3,1,2,0:T(8,128)S(1)} %broadcast_add_fusion), kind=kLoop, calls=%fused_computation.9 | loop fusion | flops 3096576 | bytes 7274496 | tf_op jit(solution)/shard_map/add | solution.py:67
  87.6 2.4 %fusion.5 = f32[4,24,8,512]{3,1,2,0:T(8,128)S(1)} fusion(f32[4,24,9,512]{3,1,2,0:T(8,128)S(1)} %fusion, f32[4,24,8,512]{3,1,2,0:T(8,128)S(1)} %get-tuple-element.154, f32[4,24,8,511]{3,1,2,0:T(8,128)S(1)} %bitcast.61, f32[4,24,8,1]{3,1,2,0:T(8,128)S(1)} %slice.778, f32[4,24,8,512]{3,1,2,0:T(8,128)S(1)} %get-tuple-element.153, ...), kind=kLoop, calls=%fused_computation.19 | loop fusion | flops 3145728 | bytes 12582912 | tf_op jit(solution)/shard_map/sub | solution.py:74
  90.1 0.5 slice.805
  90.5 0.3 slice.813
  90.9 0.5 collective-permute-start.6
  91.5 3.1 %collective-permute-start.7 = (f32[4,24,1,512]{3,1,2,0:T(8,128)S(1)}, f32[4,24,1,512]{3,1,2,0:T(8,128)S(1)}, u32[]{:S(2)}, u32[]{:S(2)}) collective-permute-start(f32[4,24,1,512]{3,1,2,0:T(8,128)S(1)} %get-tuple-element.151), channel_id=1, source_target_pairs={{4,0},{8,4},{12,8},{16,12},{20,16},{24,20},{28,24},{0,28},{5,1},{9... | collective-permute-start | bytes 589832 | tf_op jit(solution)/shard_map/ppermute | solution.py:39
  94.5 1.1 fusion.11
  95.6 0.2 slice.807
  95.9 3.8 %collective-permute-done.6 = f32[4,24,1,512]{3,1,2,0:T(8,128)S(1)} collective-permute-done((f32[4,24,1,512]{3,1,2,0:T(8,128)S(1)}, f32[4,24,1,512]{3,1,2,0:T(8,128)S(1)}, u32[]{:S(2)}, u32[]{:S(2)}) %collective-permute-start.6) | collective-permute-done | bytes 196640 | tf_op jit(solution)/shard_map/ppermute | solution.py:37
  99.7 0.5 fusion.1
  100.2 1.4 %fusion.3 = f32[4,24,8,512]{3,1,2,0:T(8,128)S(1)} fusion(f32[4,24,9,512]{3,1,2,0:T(8,128)S(1)} %fusion.1, f32[4,24,8,512]{3,1,2,0:T(8,128)S(1)} %fusion.5, f32[4,24,8,512]{3,1,2,0:T(8,128)S(1)} %get-tuple-element.150, f32[4,24,8,511]{3,1,2,0:T(8,128)S(1)} %bitcast.60, f32[4,24,8,1]{3,1,2,0:T(8,128)S(1)} %slice.807, ...), kind=kLoop, calls=%fused_computation.16 | loop fusion | flops 3145728 | bytes 12582912 | tf_op jit(solution)/shard_map/sub | solution.py:74
  101.7 0.9 convolution_bitcast_fusion
  102.6 14.8 %psum.7 = f32[3,8,512]{2,0,1:T(4,128)S(1)} all-reduce(f32[3,8,512]{2,0,1:T(4,128)S(1)} %convolution_bitcast_fusion), channel_id=1, replica_groups=mesh['space'=8,'spec'=4] {'spec'}, use_global_device_ids=true, to_apply=%region_9.10 | all-reduce | flops 12288 | bytes 98304 | tf_op jit(solution)/shard_map/psum | solution.py:145
  117.6 0.5 collective-permute-start.9
  118.2 0.7 collective-permute-done.8
  119.0 3.6 %collective-permute-done.9 = f32[3,1,512]{2,0,1:T(4,128)S(1)} collective-permute-done((f32[3,1,512]{2,0,1:T(4,128)S(1)}, f32[3,1,512]{2,0,1:T(4,128)S(1)}, u32[]{:S(2)}, u32[]{:S(2)}) %collective-permute-start.9) | collective-permute-done | bytes 6176 | tf_op jit(solution)/shard_map/ppermute | solution.py:37
  123.7 5.0 %copy.148 = f32[2,9,2,512,2]{4,3,0,2,1:T(8,128)} copy(f32[2,9,2,512,2]{3,0,1,4,2:T(2,128)S(1)} %fusion.26) | data formatting | bytes 294912 | tf_op jit(solution)/shard_map/scatter-add | solution.py:159
  128.8 7.7 %reshape.1000 = f32[2,18,1024]{2,0,1:T(2,128)S(1)} reshape(f32[2,9,2,512,2]{4,3,0,2,1:T(8,128)} %copy.148) | data formatting | bytes 294912 | tf_op jit(solution)/shard_map/reshape | solution.py:160
  136.5 2.1 %copy.149 = f32[4,24,8,512]{3,2,1,0:T(8,128)} copy(f32[4,24,8,512]{3,1,2,0:T(8,128)S(1)} %fusion.3) | data formatting | bytes 3145728
  138.6 3.1 %collective-permute-done.10 = f32[2,16,256]{2,0,1:T(2,128)S(1)} collective-permute-done((f32[2,16,256]{2,0,1:T(2,128)S(1)}, f32[2,16,256]{2,0,1:T(2,128)S(1)}, u32[]{:S(2)}, u32[]{:S(2)}) %collective-permute-start.10) | collective-permute-done | bytes 32800 | tf_op jit(solution)/shard_map/ppermute | solution.py:27
  141.7 0.6 copy.150
  (140 shorter events, 3.6 us)
Async XLA Ops:
  2.1 9.9 %copy-start.9 = (s32[12,512,4]{1,2,0:T(4,128)S(1)}, s32[12,512,4]{1,2,0:T(4,128)}, u32[]{:S(2)}) copy-start(s32[12,512,4]{1,2,0:T(4,128)} %param.30) | copy-start | bytes 294916
  2.2 10.3 %copy-start.29 = (f32[16]{0:T(128)S(1)}, f32[16]{0:T(128)}, u32[]{:S(2)}) copy-start(f32[16]{0:T(128)} %param.29) | copy-start | bytes 196
  2.2 11.1 %copy-start.30 = (f32[16]{0:T(128)S(1)}, f32[16]{0:T(128)}, u32[]{:S(2)}) copy-start(f32[16]{0:T(128)} %param.28) | copy-start | bytes 196
  2.2 11.2 %collective-permute-start = (f32[2,16,256]{2,0,1:T(2,128)S(1)}, f32[2,16,256]{2,0,1:T(2,128)S(1)}, u32[]{:S(2)}, u32[]{:S(2)}) collective-permute-start(f32[2,16,256]{2,0,1:T(2,128)S(1)} %copy_multiply_fusion), channel_id=1, source_target_pairs={{0,1},{1,2},{2,3},{3,0},{4,5},{5,6},{6,7},{7,4},{8,9},{9,10},{10,1... | collective-permute-start | bytes 98312 | tf_op jit(solution)/shard_map/ppermute | solution.py:18
  7.5 19.0 %copy-start = (f32[4,24,8,512]{3,1,2,0:T(8,128)}, f32[4,24,8,512]{3,1,2,0:T(8,128)S(1)}, u32[]{:S(2)}) copy-start(f32[4,24,8,512]{3,1,2,0:T(8,128)S(1)} %copy.134) | copy-start | bytes 4718596
  7.5 15.5 %copy-start.4 = (f32[2,16,256]{2,1,0:T(8,128)S(1)}, f32[2,16,256]{2,1,0:T(8,128)}, u32[]{:S(2)}) copy-start(f32[2,16,256]{2,1,0:T(8,128)} %param.26) | copy-start | bytes 98308
  7.5 15.7 %copy-start.10 = (f32[12,512,4]{1,2,0:T(4,128)S(1)}, f32[12,512,4]{1,2,0:T(4,128)}, u32[]{:S(2)}) copy-start(f32[12,512,4]{1,2,0:T(4,128)} %param.31) | copy-start | bytes 294916
  8.3 77.0 %collective-permute-start.4 = (f32[4,24,1,512]{3,1,2,0:T(8,128)}, f32[4,24,1,512]{3,1,2,0:T(8,128)}, u32[]{:S(2)}, u32[]{:S(2)}) collective-permute-start(f32[4,24,1,512]{3,1,2,0:T(8,128)} %get-tuple-element.156), channel_id=1, source_target_pairs={{0,4},{4,8},{8,12},{12,16},{16,20},{20,24},{24,28},{28,0},{1,5},{5... | collective-permute-start | bytes 589832 | tf_op jit(solution)/shard_map/ppermute | solution.py:37
  8.3 77.0 %collective-permute-start.5 = (f32[4,24,1,512]{3,1,2,0:T(8,128)}, f32[4,24,1,512]{3,1,2,0:T(8,128)}, u32[]{:S(2)}, u32[]{:S(2)}) collective-permute-start(f32[4,24,1,512]{3,1,2,0:T(8,128)} %get-tuple-element.155), channel_id=1, source_target_pairs={{4,0},{8,4},{12,8},{16,12},{20,16},{24,20},{28,24},{0,28},{5,1},{9... | collective-permute-start | bytes 589832 | tf_op jit(solution)/shard_map/ppermute | solution.py:39
  11.9 7.5 %copy-start.23 = (f32[24]{0:T(128)}, f32[24]{0:T(128)S(1)}, u32[]{:S(2)}) copy-start(f32[24]{0:T(128)S(1)} %get-tuple-element.196) | copy-start | bytes 292
  11.9 7.5 %copy-start.27 = (f32[24]{0:T(128)}, f32[24]{0:T(128)S(1)}, u32[]{:S(2)}) copy-start(f32[24]{0:T(128)S(1)} %get-tuple-element.197) | copy-start | bytes 292
  12.0 7.4 %copy-start.25 = (f32[24]{0:T(128)}, f32[24]{0:T(128)S(1)}, u32[]{:S(2)}) copy-start(f32[24]{0:T(128)S(1)} %fusion.46) | copy-start | bytes 292
  13.4 4.8 %collective-permute-start.1 = (f32[2,16,256]{2,0,1:T(2,128)S(1)}, f32[2,16,256]{2,0,1:T(2,128)S(1)}, u32[]{:S(2)}, u32[]{:S(2)}) collective-permute-start(f32[2,16,256]{2,0,1:T(2,128)S(1)} %collective-permute-done), channel_id=1, source_target_pairs={{0,1},{1,2},{2,3},{3,0},{4,5},{5,6},{6,7},{7,4},{8,9},{9,10},{10,1... | collective-permute-start | bytes 98312 | tf_op jit(solution)/shard_map/ppermute | solution.py:18
  18.2 4.8 %collective-permute-start.2 = (f32[2,16,256]{2,0,1:T(2,128)S(1)}, f32[2,16,256]{2,0,1:T(2,128)S(1)}, u32[]{:S(2)}, u32[]{:S(2)}) collective-permute-start(f32[2,16,256]{2,0,1:T(2,128)S(1)} %collective-permute-done.1), channel_id=1, source_target_pairs={{0,1},{1,2},{2,3},{3,0},{4,5},{5,6},{6,7},{7,4},{8,9},{9,10},{10,1... | collective-permute-start | bytes 98312 | tf_op jit(solution)/shard_map/ppermute | solution.py:18
  23.2 13.1 %collective-permute-start.3 = (f32[2,16,1024]{2,0,1:T(2,128)S(1)}, f32[2,16,1024]{2,0,1:T(2,128)}, u32[]{:S(2)}, u32[]{:S(2)}) collective-permute-start(f32[2,16,1024]{2,0,1:T(2,128)S(1)} %constant_dynamic-slice_fusion), channel_id=1, source_target_pairs={{4,0},{8,4},{12,8},{16,12},{20,16},{24,20},{28,24},{0,28},{5,1},{9... | collective-permute-start | bytes 393224 | tf_op jit(solution)/shard_map/ppermute | solution.py:27
  25.1 1.4 %slice-start.1 = ((f32[4,24,8,512]{3,2,1,0:T(8,128)}), f32[4,1,8,512]{3,2,1,0:T(8,128)S(1)}, s32[]{:S(2)}) async-start(f32[4,24,8,512]{3,2,1,0:T(8,128)} %param.25), calls=%async_computation.1 | async-start | bytes 131072 | tf_op jit(solution)/shard_map/jit(_roll_static)/slice | solution.py:72
  57.2 22.1 %copy-start.5 = (f32[12,512]{1,0:T(8,128)S(1)}, f32[12,512]{1,0:T(8,128)}, u32[]{:S(2)}) copy-start(f32[12,512]{1,0:T(8,128)} %get-tuple-element.139) | copy-start | bytes 73732
  57.2 22.1 %copy-start.6 = (f32[12,512]{1,0:T(8,128)S(1)}, f32[12,512]{1,0:T(8,128)}, u32[]{:S(2)}) copy-start(f32[12,512]{1,0:T(8,128)} %get-tuple-element.140) | copy-start | bytes 73732
  57.2 22.1 %copy-start.7 = (f32[12,512]{1,0:T(8,128)S(1)}, f32[12,512]{1,0:T(8,128)}, u32[]{:S(2)}) copy-start(f32[12,512]{1,0:T(8,128)} %get-tuple-element.141) | copy-start | bytes 73732
  57.2 22.1 %copy-start.8 = (f32[12,512]{1,0:T(8,128)S(1)}, f32[12,512]{1,0:T(8,128)}, u32[]{:S(2)}) copy-start(f32[12,512]{1,0:T(8,128)} %get-tuple-element.142) | copy-start | bytes 73732
  78.8 1.3 copy-start.24
  78.9 1.3 copy-start.26
  78.9 1.3 copy-start.28
  79.3 1.2 copy-start.21
  80.7 1.4 copy-start.2
  80.7 1.9 %copy-start.3 = (f32[4,23,8,512]{3,1,2,0:T(8,128)S(1)}, f32[4,23,8,512]{3,1,2,0:T(8,128)}, u32[]{:S(2)}) copy-start(f32[4,23,8,512]{3,1,2,0:T(8,128)} %slice.802) | copy-start | bytes 4521988
  81.2 1.6 %slice-start = ((f32[4,24,8,512]{3,1,2,0:T(8,128)}), f32[4,24,8,1]{3,1,2,0:T(8,128)S(1)}, s32[]{:S(2)}) async-start(f32[4,24,8,512]{3,1,2,0:T(8,128)} %copy-done), calls=%async_computation | async-start | bytes 786432 | tf_op jit(solution)/shard_map/jit(_roll_static)/slice | solution.py:64
  82.8 2.2 %copy-start.22 = (f32[4,24]{1,0:T(4,128)S(1)}, f32[4,24]{1,0:T(4,128)}, u32[]{:S(2)}) copy-start(f32[4,24]{1,0:T(4,128)} %get-tuple-element.190) | copy-start | bytes 1156
  84.7 1.4 copy-start.1
  90.9 8.7 %collective-permute-start.6 = (f32[4,24,1,512]{3,1,2,0:T(8,128)S(1)}, f32[4,24,1,512]{3,1,2,0:T(8,128)S(1)}, u32[]{:S(2)}, u32[]{:S(2)}) collective-permute-start(f32[4,24,1,512]{3,1,2,0:T(8,128)S(1)} %get-tuple-element.152), channel_id=1, source_target_pairs={{0,4},{4,8},{8,12},{12,16},{16,20},{20,24},{24,28},{28,0},{1,5},{5... | collective-permute-start | bytes 589832 | tf_op jit(solution)/shard_map/ppermute | solution.py:37
  91.5 8.2 %collective-permute-start.7 = (f32[4,24,1,512]{3,1,2,0:T(8,128)S(1)}, f32[4,24,1,512]{3,1,2,0:T(8,128)S(1)}, u32[]{:S(2)}, u32[]{:S(2)}) collective-permute-start(f32[4,24,1,512]{3,1,2,0:T(8,128)S(1)} %get-tuple-element.151), channel_id=1, source_target_pairs={{4,0},{8,4},{12,8},{16,12},{20,16},{24,20},{28,24},{0,28},{5,1},{9... | collective-permute-start | bytes 589832 | tf_op jit(solution)/shard_map/ppermute | solution.py:39
  100.2 1.5 %copy-start.20 = (f32[3,4,24]{2,1,0:T(4,128)S(1)}, f32[3,4,24]{2,1,0:T(4,128)}, u32[]{:S(2)}) copy-start(f32[3,4,24]{2,1,0:T(4,128)} %pad_maximum_fusion.6) | copy-start | bytes 3460
  101.6 21.0 %copy-start.17 = (f32[8,512]{1,0:T(8,128)S(1)}, f32[8,512]{1,0:T(8,128)}, u32[]{:S(2)}) copy-start(f32[8,512]{1,0:T(8,128)} %slice.830) | copy-start | bytes 49156
  101.6 21.0 %copy-start.18 = (f32[8,512]{1,0:T(8,128)S(1)}, f32[8,512]{1,0:T(8,128)}, u32[]{:S(2)}) copy-start(f32[8,512]{1,0:T(8,128)} %slice.838) | copy-start | bytes 49156
  101.7 21.0 %copy-start.19 = (f32[8,512]{1,0:T(8,128)S(1)}, f32[8,512]{1,0:T(8,128)}, u32[]{:S(2)}) copy-start(f32[8,512]{1,0:T(8,128)} %slice.846) | copy-start | bytes 49156
  101.7 21.3 %copy-start.16 = (f32[8,512]{1,0:T(8,128)S(1)}, f32[8,512]{1,0:T(8,128)}, u32[]{:S(2)}) copy-start(f32[8,512]{1,0:T(8,128)} %slice.817) | copy-start | bytes 49156
  101.7 21.4 %copy-start.15 = (f32[8,512]{1,0:T(8,128)S(1)}, f32[8,512]{1,0:T(8,128)}, u32[]{:S(2)}) copy-start(f32[8,512]{1,0:T(8,128)} %slice.828) | copy-start | bytes 49156
  101.7 21.5 %copy-start.14 = (f32[8,512]{1,0:T(8,128)S(1)}, f32[8,512]{1,0:T(8,128)}, u32[]{:S(2)}) copy-start(f32[8,512]{1,0:T(8,128)} %slice.834) | copy-start | bytes 49156
  101.7 21.6 %copy-start.13 = (f32[8,512]{1,0:T(8,128)S(1)}, f32[8,512]{1,0:T(8,128)}, u32[]{:S(2)}) copy-start(f32[8,512]{1,0:T(8,128)} %slice.836) | copy-start | bytes 49156
  101.7 21.8 %copy-start.12 = (f32[8,512]{1,0:T(8,128)S(1)}, f32[8,512]{1,0:T(8,128)}, u32[]{:S(2)}) copy-start(f32[8,512]{1,0:T(8,128)} %slice.842) | copy-start | bytes 49156
  101.7 21.8 %copy-start.11 = (f32[8,512]{1,0:T(8,128)S(1)}, f32[8,512]{1,0:T(8,128)}, u32[]{:S(2)}) copy-start(f32[8,512]{1,0:T(8,128)} %slice.844) | copy-start | bytes 49156
  117.6 1.4 collective-permute-start.8
  117.6 4.9 %collective-permute-start.9 = (f32[3,1,512]{2,0,1:T(4,128)S(1)}, f32[3,1,512]{2,0,1:T(4,128)S(1)}, u32[]{:S(2)}, u32[]{:S(2)}) collective-permute-start(f32[3,1,512]{2,0,1:T(4,128)S(1)} %get-tuple-element.170), channel_id=1, source_target_pairs={{0,4},{4,8},{8,12},{12,16},{16,20},{20,24},{24,28},{28,0},{1,5},{5... | collective-permute-start | bytes 18440 | tf_op jit(solution)/shard_map/ppermute | solution.py:37
  136.5 5.2 %collective-permute-start.10 = (f32[2,16,256]{2,0,1:T(2,128)S(1)}, f32[2,16,256]{2,0,1:T(2,128)S(1)}, u32[]{:S(2)}, u32[]{:S(2)}) collective-permute-start(f32[2,16,256]{2,0,1:T(2,128)S(1)} %pad_dynamic-slice_fusion.1), channel_id=1, source_target_pairs={{28,0},{0,4},{4,8},{8,12},{12,16},{16,20},{20,24},{24,28},{29,1},{... | collective-permute-start | bytes 98312 | tf_op jit(solution)/shard_map/ppermute | solution.py:27
